TPU v7x, 32 devices: a whole 2x2x4 slice. The times are simulated.
32 devices in a mesh: ctx: 4 (over z), exp: 4 (over y, x), head: 2 (over core).
Axes of the slice: x: 2, y: 2, z: 4, core: 2. Of those that a mesh axis runs over, the one named last changes fastest.
Arguments:
- queries: bfloat16 [2048, 2048], P(('ctx', 'exp'), 'head'), may hold values from -6 to 6
- keys: bfloat16 [2048, 256], P(('ctx', 'exp'), 'head'), may hold values from -6 to 6
- values: bfloat16 [2048, 256], P(('ctx', 'exp'), 'head'), may hold values from -12 to 12
- residual: bfloat16 [2048, 2880], P(('ctx', 'exp', 'head')), may hold values from -48 to 48
- out_projection: bfloat16 [2048, 2880], P('head', 'exp'), may hold values from -0.125 to 0.125
- norm_gain: float32 [2880], replicated, may hold values from 0.25 to 1.75
- route_ids: int32 [2048, 4], P(('ctx', 'exp', 'head')), may hold values from 0 to 7, all different within a row; in each aligned block of 64 rows (0 to 63, 64 to 127, ...) at most 64 rows name the same one
- route_weights: float32 [2048, 4], P(('ctx', 'exp', 'head')), may hold values from 0.05 to 1
- w_gate: bfloat16 [8, 2880, 1536], P(('ctx', 'head'), None, 'exp'), may hold values from -0.109375 to 0.109375
- w_up: bfloat16 [8, 2880, 1536], P(('ctx', 'head'), None, 'exp'), may hold values from -0.109375 to 0.109375
- w_down: bfloat16 [8, 1536, 2880], P(('ctx', 'head'), 'exp'), may hold values from -0.15625 to 0.15625
Outputs:
- mixed: bfloat16 [2048, 2880], P(('ctx', 'exp', 'head'))
Inputs may be any that keep to these rules, and one draw needn't show every extreme that they name: `route_ids`: each row names 4 different experts. In the rows of one device (aligned blocks of 64 rows) no expert is named by more than 64 rows, a bound that some block reaches.
All inputs are finite; a program needn't handle non-finite values.
Results may differ from a plain program's by a relative error of at most 0.0037.
Values may be sent and summed in bfloat16 or wider, within the bound.
No kernel may reach another device: no remote copies, remote signals or barrier semaphores. Data moves between devices by JAX's collectives and lax.ppermute only.
A program may use at most 128 MiB of HBM per device.

v0:
```python
import jax
import jax.numpy as jnp
from jax import lax
from jax.sharding import PartitionSpec as P

D = 2880
QUERY_HEADS = 32
KEY_VALUE_HEADS = 4
HEAD_DIMENSION = 64
BAND_WIDTH_KEYS = 128
TOP = 4
EPSILON = 1e-05
SLOPE = 1.702


def from_behind(x, axis, by):
    devices = lax.axis_size(axis)
    pairs = [(i, i + by) for i in range(devices) if 0 <= i + by < devices]
    return lax.ppermute(x, axis, pairs)


def attend_band(
    queries, concatenated_keys, concatenated_values, window, head_size, group, anchor_position
):
    tokens = queries.shape[0]
    block = min(tokens, 512)
    count = tokens // block
    heads = queries.shape[1] // head_size
    kv_heads = heads // group
    scale = head_size ** (-0.5)

    def one_block(index):
        begin = index * block
        query_part = queries.reshape(block, kv_heads, group, head_size)
        key_part = concatenated_keys.reshape(block + window, kv_heads, head_size)
        value_part = concatenated_values.reshape(block + window, kv_heads, head_size)
        scores = (
            jnp.einsum("qgjd,kgd->gjqk", query_part, key_part, preferred_element_type=jnp.float32)
            * scale
        )
        query_pos = anchor_position + begin + jnp.arange(block, dtype=jnp.int32)
        key_pos = anchor_position - window + begin + jnp.arange(block + window, dtype=jnp.int32)
        distance = query_pos[:, None] - key_pos[None, :]
        allowed = (distance >= 0) & (distance < window) & (key_pos[None, :] >= 0)
        scores = jnp.where(allowed, scores, -jnp.inf)
        highest = jnp.max(scores, axis=-1, keepdims=True)
        weights = jnp.exp(scores - highest)
        weights = (weights / jnp.sum(weights, axis=-1, keepdims=True)).astype(jnp.bfloat16)
        result = jnp.einsum(
            "gjqk,kgd->qgjd", weights, value_part, preferred_element_type=jnp.float32
        )
        return result.astype(jnp.bfloat16).reshape(block, heads * head_size)

    outputs = lax.map(one_block, jnp.arange(count, dtype=jnp.int32))
    return outputs.reshape(tokens, heads * head_size)


def expert_rows(inputs, gate_slice, up_slice, down_slice):
    gate = jnp.dot(inputs, gate_slice, preferred_element_type=jnp.float32)
    upward = jnp.dot(inputs, up_slice, preferred_element_type=jnp.float32)
    active = ((upward + 1.0) * gate * jax.nn.sigmoid(SLOPE * gate)).astype(jnp.bfloat16)
    return jnp.dot(active, down_slice, preferred_element_type=jnp.float32)


def local(
    queries,
    keys,
    values,
    residual,
    out_projection,
    norm_gain,
    route_ids,
    route_weights,
    w_gate,
    w_up,
    w_down,
):
    tokens = queries.shape[0]
    key_band_extent = keys.shape[1]
    stacked = jnp.concatenate([keys, values], axis=1)
    prior = from_behind(stacked, ("ctx", "exp"), 1)
    joined_heads = jnp.concatenate([prior, stacked], axis=0)
    anchor_position = lax.axis_index(("ctx", "exp")) * tokens
    attended_rows = attend_band(
        queries,
        joined_heads[:, :key_band_extent],
        joined_heads[:, key_band_extent:],
        BAND_WIDTH_KEYS,
        HEAD_DIMENSION,
        QUERY_HEADS // KEY_VALUE_HEADS,
        anchor_position,
    )
    partial_sum = jnp.dot(
        attended_rows,
        lax.all_gather(out_projection, "exp", axis=1, tiled=True),
        preferred_element_type=jnp.float32,
    )
    attn_out = lax.psum_scatter(partial_sum, "head", scatter_dimension=0, tiled=True)
    hidden_state = residual.astype(jnp.float32) + attn_out
    mean_square = jnp.mean(hidden_state * hidden_state, axis=1, keepdims=True)
    normed = (hidden_state * lax.rsqrt(mean_square + EPSILON) * norm_gain[None, :]).astype(
        jnp.bfloat16
    )
    local_rows = normed.shape[0]
    experts = lax.axis_size("ctx") * lax.axis_size("head")
    capacity = max(2, TOP * tokens // experts)
    flat_ids = route_ids.reshape(-1)
    one_hot = (flat_ids[:, None] == jnp.arange(experts, dtype=jnp.int32)[None, :]).astype(jnp.int32)
    earlier = jnp.cumsum(one_hot, axis=0) - one_hot
    rank = jnp.sum(earlier * one_hot, axis=1)
    slot = flat_ids * capacity + rank
    outgoing = (
        jnp.zeros((experts * capacity, D), jnp.bfloat16)
        .at[slot]
        .set(jnp.repeat(normed, TOP, axis=0))
    )
    outgoing = outgoing.reshape(experts, capacity, D)
    arrived = lax.all_to_all(outgoing, ("ctx", "head"), split_axis=0, concat_axis=0, tiled=True)
    pooled = lax.all_gather(arrived, "exp", axis=0, tiled=True)
    partial_rows = expert_rows(
        pooled.reshape(experts * lax.axis_size("exp") * capacity, D), w_gate[0], w_up[0], w_down[0]
    )
    summed = lax.psum_scatter(
        partial_rows.reshape(experts * lax.axis_size("exp"), capacity, D),
        "exp",
        scatter_dimension=0,
        tiled=True,
    ).astype(jnp.bfloat16)
    returned = lax.all_to_all(summed, ("ctx", "head"), split_axis=0, concat_axis=0, tiled=True)
    flat_back = returned.reshape(experts * capacity, D)
    picked = flat_back[slot].astype(jnp.float32).reshape(local_rows, TOP, D)
    moe = jnp.sum(picked * route_weights[:, :, None], axis=1)
    return (hidden_state + moe).astype(jnp.bfloat16)


def solution(mesh):
    return jax.shard_map(
        local,
        mesh=mesh,
        in_specs=(
            P(("ctx", "exp"), "head"),
            P(("ctx", "exp"), "head"),
            P(("ctx", "exp"), "head"),
            P(("ctx", "exp", "head"), None),
            P("head", "exp"),
            P(),
            P(("ctx", "exp", "head"), None),
            P(("ctx", "exp", "head"), None),
            P(("ctx", "head"), None, "exp"),
            P(("ctx", "head"), None, "exp"),
            P(("ctx", "head"), "exp", None),
        ),
        out_specs=P(("ctx", "exp", "head"), None),
        check_vma=False,
    )
```

profile of v0, /device:TPU:0, one launch (start us, length us, event | category | flops | bytes accessed | tf_op | source)
XLA Modules:
  0.0 637.0 jit_solution(17359367700430694004)
XLA Ops:
  6.5 0.7 all-gather.3.cloned.1.call-update
  7.3 0.8 constant_dynamic-update-slice_fusion.1
  8.1 0.8 constant_dynamic-update-slice_fusion
  8.8 4.9 collective-permute-start
  13.9 1.1 copy.27
  15.0 0.6 collective-permute-done
  15.8 0.8 fusion.26
  16.6 1.1 convolution_convert_fusion
  17.7 61.0 %all-gather.3.cloned.1.call-done = bf16[1024,2880]{0,1:T(8,128)(2,1)} async-done(((bf16[1024,720]{0,1:T(8,128)(2,1)}), bf16[1024,2880]{0,1:T(8,128)(2,1)}) %all-gather.3.cloned.1.call-update) | async-done | bytes 5898256 | tf_op jit(solution)/shard_map/all_gather | solution.py:95
  78.7 6.0 fusion.27
  85.1 0.6 reduce-window.6
  85.7 0.2 slice_reduce_fusion
  86.2 7.6 %reduce-scatter.3.cloned.1.call-done = f32[64,2880]{1,0:T(8,128)} async-done(((f32[128,2880]{1,0:T(8,128)}), f32[64,2880]{1,0:T(8,128)}) %reduce-scatter.3.cloned.1.call-update) | async-done | bytes 737296 | tf_op jit(solution)/shard_map/reduce_scatter | solution.py:98
  93.8 1.3 multiply_reduce_fusion.1
  95.2 1.3 multiply_convert_fusion.1
  96.4 1.5 broadcast_in_dim.38
  98.0 3.6 reshape.129
  101.5 5.6 scatter_custom_fusion
  107.1 73.8 %all_to_all.10 = bf16[8,64,2880]{2,1,0:T(8,128)(2,1)} all-to-all(bf16[8,64,2880]{2,1,0:T(8,128)(2,1)} %bitcast.60), channel_id=1, replica_groups=mesh['ctx'=4,'exp'=4,'head'=2] {'ctx','head'}, dimensions={0} | all-to-all | bytes 5898240 | tf_op jit(solution)/shard_map/all_to_all | solution.py:118
  180.9 0.2 reduce-scatter.5.cloned.1.call-start
  181.1 116.8 %all-gather.5.cloned.1.call-done = bf16[32,64,2880]{2,1,0:T(8,128)(2,1)} async-done(((bf16[8,64,2880]{2,1,0:T(8,128)(2,1)}), bf16[32,64,2880]{2,1,0:T(8,128)(2,1)}) %all-gather.5.cloned.1.call-update) | async-done | bytes 11796496 | tf_op jit(solution)/shard_map/all_gather | solution.py:119
  298.0 10.6 %fusion.3 = f32[2048,384]{1,0:T(8,128)S(1)} fusion(bf16[2048,2880]{1,0:T(8,128)(2,1)} %bitcast.71, bf16[1,2880,384]{2,1,0:T(8,128)(2,1)} %param.19), kind=kOutput, calls=%fused_computation.7 | convolution fusion | flops 4529848320 | bytes 17154048 | tf_op jit(solution)/shard_map/dot_general | solution.py:59
  308.6 7.3 %multiply_convert_fusion = bf16[2048,384]{1,0:T(8,128)(2,1)S(1)} fusion(f32[2048,384]{1,0:T(8,128)S(1)} %fusion.3, bf16[2048,2880]{1,0:T(8,128)(2,1)S(1)} %bitcast.72, bf16[1,2880,384]{2,1,0:T(8,128)(2,1)S(1)} %copy-done.8), kind=kOutput, calls=%fused_computation.3 | convolution fusion | flops 4536139776 | bytes 18726912 | tf_op jit(solution)/shard_map/dot_general | solution.py:60
  315.9 11.4 %fusion.1 = f32[32,64,2880]{2,1,0:T(8,128)} fusion(bf16[32,64,384]{2,1,0:T(8,128)(2,1)S(1)} %bitcast.61, bf16[1,384,2880]{1,2,0:T(8,128)(2,1)S(1)} %copy-done), kind=kOutput, calls=%fused_computation.5 | convolution fusion | flops 4529848320 | bytes 27377664 | tf_op jit(solution)/shard_map/dot_general | solution.py:62
  327.3 213.4 %reduce-scatter.5.cloned.1.call-done = f32[8,64,2880]{2,1,0:T(8,128)} async-done(((f32[32,64,2880]{2,1,0:T(8,128)}), f32[8,64,2880]{2,1,0:T(8,128)}) %reduce-scatter.5.cloned.1.call-update) | async-done | bytes 5898256 | tf_op jit(solution)/shard_map/reduce_scatter | solution.py:123
  540.7 4.8 convert_element_type.48
  545.4 4.7 all-to-all-start.1
  550.3 68.6 %all-to-all-done.1 = bf16[8,64,2880]{2,1,0:T(8,128)(2,1)S(1)} async-done(((bf16[8,64,2880]{2,1,0:T(8,128)(2,1)}), bf16[8,64,2880]{2,1,0:T(8,128)(2,1)S(1)}, u32[]{:S(2)}, u32[]{:S(2)}) %all-to-all-start.1) | async-done | bytes 2949152 | tf_op jit(solution)/shard_map/all_to_all | solution.py:129
  618.9 2.7 gather_fusion
  621.5 4.1 reshape.116
  625.6 4.0 multiply_reduce_fusion
  629.6 0.9 add_convert_fusion
  (45 shorter events, 1.3 us)
Async XLA Ops:
  6.5 309.3 %copy-start = (bf16[1,384,2880]{1,2,0:T(8,128)(2,1)S(1)}, bf16[1,384,2880]{1,2,0:T(8,128)(2,1)}, u32[]{:S(2)}) copy-start(bf16[1,384,2880]{1,2,0:T(8,128)(2,1)} %param.21) | copy-start | bytes 6635524
  6.5 72.2 %all-gather.3.cloned.1.call-start = ((), (), s32[]{:S(2)}) async-start(), calls=%async_computation.4 | async-start | bytes 7372800 | tf_op jit(solution)/shard_map/all_gather | solution.py:95
  7.3 86.6 %reduce-scatter.3.cloned.1.call-start = ((), (), s32[]{:S(2)}) async-start(), calls=%async_computation.5 | async-start | bytes 2260992 | tf_op jit(solution)/shard_map/reduce_scatter | solution.py:98
  8.8 6.8 %collective-permute-start = (bf16[128,256]{1,0:T(8,128)(2,1)S(1)}, bf16[128,256]{1,0:T(8,128)(2,1)S(1)}, u32[]{:S(2)}, u32[]{:S(2)}) collective-permute-start(bf16[128,256]{1,0:T(8,128)(2,1)S(1)} %constant_dynamic-update-slice_fusion), channel_id=1, source_target_pairs={{0,2},{2,4},{4,6},{6,8},{8,10},{10,12},{12,14},{14,16},{16,18},{18... | collective-permute-start | bytes 196616 | tf_op jit(solution)/shard_map/ppermute | solution.py:19
  78.7 6.1 copy-start.5
  78.7 15.1 %copy-start.3 = (bf16[64,2880]{1,0:T(8,128)(2,1)S(1)}, bf16[64,2880]{1,0:T(8,128)(2,1)}, u32[]{:S(2)}) copy-start(bf16[64,2880]{1,0:T(8,128)(2,1)} %param.14) | copy-start | bytes 1105924
  84.7 10.5 %copy-start.4 = (f32[2880]{0:T(1024)S(1)}, f32[2880]{0:T(1024)}, u32[]{:S(2)}) copy-start(f32[2880]{0:T(1024)} %param.16) | copy-start | bytes 34564
  84.7 213.3 %all-gather.5.cloned.1.call-start = ((), (), s32[]{:S(2)}) async-start(), calls=%async_computation.6 | async-start | bytes 15073280 | tf_op jit(solution)/shard_map/all_gather | solution.py:119
  180.9 359.7 %reduce-scatter.5.cloned.1.call-start = ((), (), s32[]{:S(2)}) async-start(), calls=%async_computation.7 | async-start | bytes 30146560 | tf_op jit(solution)/shard_map/reduce_scatter | solution.py:123
  298.0 10.6 %copy-start.7 = (bf16[32,64,2880]{2,1,0:T(8,128)(2,1)S(1)}, bf16[32,64,2880]{2,1,0:T(8,128)(2,1)}, u32[]{:S(2)}) copy-start(bf16[32,64,2880]{2,1,0:T(8,128)(2,1)} %all-gather.5.cloned.1.call-done) | copy-start | bytes 35389444
  298.0 10.6 %copy-start.8 = (bf16[1,2880,384]{2,1,0:T(8,128)(2,1)S(1)}, bf16[1,2880,384]{2,1,0:T(8,128)(2,1)}, u32[]{:S(2)}) copy-start(bf16[1,2880,384]{2,1,0:T(8,128)(2,1)} %param.20) | copy-start | bytes 6635524
  545.4 4.7 copy-start.6
  545.4 73.4 %all-to-all-start.1 = ((bf16[8,64,2880]{2,1,0:T(8,128)(2,1)}), bf16[8,64,2880]{2,1,0:T(8,128)(2,1)S(1)}, u32[]{:S(2)}, u32[]{:S(2)}) async-start(bf16[8,64,2880]{2,1,0:T(8,128)(2,1)} %convert_element_type.48), calls=%async_computation.3 | async-start | bytes 6029312 | tf_op jit(solution)/shard_map/all_to_all | solution.py:129
  621.5 8.9 %copy-start.1 = (bf16[1,384,2880]{1,2,0:T(8,128)(2,1)S(1)}, bf16[1,384,2880]{1,2,0:T(8,128)(2,1)}, u32[]{:S(2)}) copy-start(bf16[1,384,2880]{1,2,0:T(8,128)(2,1)} %param.21) | copy-start | bytes 6635524
  625.6 4.0 copy-start.2
Sparse Core Ops, SparseCore 0:
  9.2 69.4 all-gather.2
  84.8 8.9 reduce-scatter.2
  181.0 116.8 all-gather.4
  327.4 213.2 reduce-scatter.4
where the time goes:
time: 638 us; the launch traced here: 637 us
  waiting for transfers between devices  469 us (74%)
  blocking collectives  73.8 us (12%)
  matrix products  37.1 us (6%)
  local copies, waits for them, and re-layouts  21.2 us (3%)
  between operations  13.3 us (2%)
  other arithmetic  13.1 us (2%)
  starting transfers between devices  9.91 us (2%)
    reduce_scatter x1, waiting for transfers between devices, local(): lax.psum_scatter(partial_rows.reshape(experts * lax.axis_size('exp'), cap...  213 us
    all_gather x1, waiting for transfers between devices, local(): pooled = lax.all_gather(arrived, 'exp', axis=0, tiled=True)  117 us
    all_to_all x1, blocking collectives, local(): lax.all_to_all(outgoing, ('ctx', 'head'), split_axis=0, concat_axis=0, ti...  73.8 us
    all_to_all x1, waiting for transfers between devices, local(): lax.all_to_all(summed, ('ctx', 'head'), split_axis=0, concat_axis=0, tile...  68.6 us
    all_gather x1, waiting for transfers between devices, local(): lax.all_gather(out_projection, 'exp', axis=1, tiled=True)  61 us
  transfers between devices with their start and end apart: 6, of which 6 were waited for; matrix products, arithmetic and copies ran while one was open for 1% of the time, Pallas kernels for 0%

commit v1 on v0

--- a/solution.py
+++ b/solution.py
@@ -11,6 +11,22 @@
 TOP = 4
 EPSILON = 1e-05
 SLOPE = 1.702
+
+
+def collect(x, axis, dim):
+    ways, here, step = (lax.axis_size(axis), lax.axis_index(axis), x.shape[dim])
+    lengths = [n * ways if d == dim else n for d, n in enumerate(x.shape)]
+    full = lax.dynamic_update_slice_in_dim(jnp.zeros(lengths, x.dtype), x, here * step, axis=dim)
+    going_up = going_down = x
+    for far in range(1, ways // 2 + 1):
+        going_up = lax.ppermute(going_up, axis, [(d, (d + 1) % ways) for d in range(ways)])
+        full = lax.dynamic_update_slice_in_dim(full, going_up, (here - far) % ways * step, axis=dim)
+        if 2 * far < ways:
+            going_down = lax.ppermute(going_down, axis, [(d, (d - 1) % ways) for d in range(ways)])
+            full = lax.dynamic_update_slice_in_dim(
+                full, going_down, (here + far) % ways * step, axis=dim
+            )
+    return full
 
 
 def from_behind(x, axis, by):
@@ -116,7 +132,7 @@
     )
     outgoing = outgoing.reshape(experts, capacity, D)
     arrived = lax.all_to_all(outgoing, ("ctx", "head"), split_axis=0, concat_axis=0, tiled=True)
-    pooled = lax.all_gather(arrived, "exp", axis=0, tiled=True)
+    pooled = collect(arrived, "exp", 0)
     partial_rows = expert_rows(
         pooled.reshape(experts * lax.axis_size("exp") * capacity, D), w_gate[0], w_up[0], w_down[0]
     )

time: 638 us -> 724 us (1.13)
  waiting for transfers between devices: 469 us -> 527 us
  local copies, waits for them, and re-layouts: 21.2 us -> 45.6 us
    ppermute x0 -> x3, waiting for transfers between devices: none -> 177 us  [the longest x2 126 us: collect(): lax.ppermute(going_up, axis, [(d, (d + 1) % ways) for d in range(ways)])]
    all_gather x1 -> x0, waiting for transfers between devices: 117 us -> none  [local(): pooled = lax.all_gather(arrived, 'exp', axis=0, tiled=True)]
    dynamic_update_slice x0 -> x4, local copies, waits for them, and re-layouts: none -> 14.8 us  [the longest x2 7.41 us: collect(): lax.dynamic_update_slice_in_dim(full, going_up, (here - far) % ways * ste...]
  transfers between devices with their start and end apart: 6 -> 8, of which waited for: 6 -> 8; matrix products, arithmetic and copies ran while one was open for 1% -> 3% of each run, Pallas kernels for 0% -> 0%
where the time goes in v1:
time: 724 us; the launch traced here: 723 us
  waiting for transfers between devices  527 us (73%)
  blocking collectives  73.8 us (10%)
  local copies, waits for them, and re-layouts  45.6 us (6%)
  matrix products  37.4 us (5%)
  between operations  13.3 us (2%)
  starting transfers between devices  13.2 us (2%)
  other arithmetic  13.2 us (2%)
    reduce_scatter x1, waiting for transfers between devices, local(): lax.psum_scatter(partial_rows.reshape(experts * lax.axis_size('exp'), cap...  212 us
    ppermute x2, waiting for transfers between devices, collect(): lax.ppermute(going_up, axis, [(d, (d + 1) % ways) for d in range(ways)])  126 us
    all_to_all x1, blocking collectives, local(): lax.all_to_all(outgoing, ('ctx', 'head'), split_axis=0, concat_axis=0, ti...  73.8 us
    all_to_all x1, waiting for transfers between devices, local(): lax.all_to_all(summed, ('ctx', 'head'), split_axis=0, concat_axis=0, tile...  68.6 us
    all_gather x1, waiting for transfers between devices, local(): lax.all_gather(out_projection, 'exp', axis=1, tiled=True)  61 us
    ppermute x1, waiting for transfers between devices, collect(): lax.ppermute(going_down, axis, [(d, (d - 1) % ways) for d in range(ways)])  50.7 us
  transfers between devices with their start and end apart: 8, of which 8 were waited for; matrix products, arithmetic and copies ran while one was open for 3% of the time, Pallas kernels for 0%

profile of v1, /device:TPU:0, one launch (start us, length us, event | category | flops | bytes accessed | tf_op | source)
XLA Modules:
  0.0 723.4 jit_solution(2656331731684412705)
XLA Ops:
  8.8 4.9 collective-permute-start
  13.9 1.1 copy.19
  16.6 1.1 convolution_convert_fusion
  17.7 61.0 %all-gather.2.cloned.1.call-done = bf16[1024,2880]{0,1:T(8,128)(2,1)} async-done(((bf16[1024,720]{0,1:T(8,128)(2,1)}), bf16[1024,2880]{0,1:T(8,128)(2,1)}) %all-gather.2.cloned.1.call-update) | async-done | bytes 5898256 | tf_op jit(solution)/shard_map/all_gather | solution.py:111
  78.7 6.0 fusion.30
  86.2 7.6 %reduce-scatter.3.cloned.1.call-done = f32[64,2880]{1,0:T(8,128)} async-done(((f32[128,2880]{1,0:T(8,128)}), f32[64,2880]{1,0:T(8,128)}) %reduce-scatter.3.cloned.1.call-update) | async-done | bytes 737296 | tf_op jit(solution)/shard_map/reduce_scatter | solution.py:114
  93.8 1.3 multiply_reduce_fusion.1
  95.2 1.3 multiply_convert_fusion.1
  96.4 1.5 broadcast_in_dim.42
  98.0 3.6 reshape.129
  101.5 5.6 scatter_custom_fusion
  107.1 73.8 %all_to_all.10 = bf16[8,64,2880]{2,1,0:T(8,128)(2,1)} all-to-all(bf16[8,64,2880]{2,1,0:T(8,128)(2,1)} %bitcast.63), channel_id=1, replica_groups=mesh['ctx'=4,'exp'=4,'head'=2] {'ctx','head'}, dimensions={0} | all-to-all | bytes 5898240 | tf_op jit(solution)/shard_map/all_to_all | solution.py:134
  180.9 1.5 collective-permute-start.1
  182.4 1.5 collective-permute-start.2
  183.8 66.5 %collective-permute-done.1 = bf16[8,64,2880]{2,1,0:T(8,128)(2,1)} collective-permute-done((bf16[8,64,2880]{2,1,0:T(8,128)(2,1)}, bf16[8,64,2880]{2,1,0:T(8,128)(2,1)}, u32[]{:S(2)}, u32[]{:S(2)}) %collective-permute-start.1) | collective-permute-done | bytes 2949152 | tf_op jit(solution)/shard_map/ppermute | solution.py:22
  250.8 6.1 broadcast_in_dim.40
  256.9 3.7 constant_dynamic-update-slice_fusion.5
  260.6 3.7 constant_dynamic-update-slice_fusion.4
  264.2 50.7 %collective-permute-done.2 = bf16[8,64,2880]{2,1,0:T(8,128)(2,1)} collective-permute-done((bf16[8,64,2880]{2,1,0:T(8,128)(2,1)}, bf16[8,64,2880]{2,1,0:T(8,128)(2,1)}, u32[]{:S(2)}, u32[]{:S(2)}) %collective-permute-start.2) | collective-permute-done | bytes 2949152 | tf_op jit(solution)/shard_map/ppermute | solution.py:25
  314.9 3.7 constant_dynamic-update-slice_fusion.3
  318.6 59.5 %collective-permute-done.3 = bf16[8,64,2880]{2,1,0:T(8,128)(2,1)} collective-permute-done((bf16[8,64,2880]{2,1,0:T(8,128)(2,1)}, bf16[8,64,2880]{2,1,0:T(8,128)(2,1)}, u32[]{:S(2)}, u32[]{:S(2)}) %collective-permute-start.3) | collective-permute-done | bytes 2949152 | tf_op jit(solution)/shard_map/ppermute | solution.py:22
  378.2 3.7 constant_dynamic-update-slice_fusion.2
  381.9 10.8 %fusion.7 = f32[2048,384]{1,0:T(8,128)S(1)} fusion(bf16[2048,2880]{1,0:T(8,128)(2,1)} %bitcast.61, bf16[1,2880,384]{2,1,0:T(8,128)(2,1)S(1)} %copy-done.7), kind=kOutput, calls=%fused_computation.9 | convolution fusion | flops 4529848320 | bytes 17154048 | tf_op jit(solution)/shard_map/dot_general | solution.py:76
  392.7 7.4 %multiply_convert_fusion = bf16[2048,384]{1,0:T(8,128)(2,1)S(1)} fusion(f32[2048,384]{1,0:T(8,128)S(1)} %fusion.7, bf16[2048,2880]{1,0:T(8,128)(2,1)S(1)} %bitcast.62, bf16[1,2880,384]{2,1,0:T(8,128)(2,1)S(1)} %copy-done.8), kind=kOutput, calls=%fused_computation.3 | convolution fusion | flops 4536139776 | bytes 18726912 | tf_op jit(solution)/shard_map/dot_general | solution.py:75
  400.2 11.4 %fusion.1 = f32[32,64,2880]{2,1,0:T(8,128)} fusion(bf16[32,64,384]{2,1,0:T(8,128)(2,1)S(1)} %bitcast.64, bf16[1,384,2880]{1,2,0:T(8,128)(2,1)S(1)} %copy-done), kind=kOutput, calls=%fused_computation.5 | convolution fusion | flops 4529848320 | bytes 27377664 | tf_op jit(solution)/shard_map/dot_general | solution.py:78
  411.6 211.7 %reduce-scatter.5.cloned.1.call-done = f32[8,64,2880]{2,1,0:T(8,128)} async-done(((f32[32,64,2880]{2,1,0:T(8,128)}), f32[8,64,2880]{2,1,0:T(8,128)}) %reduce-scatter.5.cloned.1.call-update) | async-done | bytes 5898256 | tf_op jit(solution)/shard_map/reduce_scatter | solution.py:139
  623.3 4.8 convert_element_type.48
  628.1 4.8 all-to-all-start.1
  633.0 68.6 %all-to-all-done.1 = bf16[8,64,2880]{2,1,0:T(8,128)(2,1)} async-done(((bf16[8,64,2880]{2,1,0:T(8,128)(2,1)}), bf16[8,64,2880]{2,1,0:T(8,128)(2,1)}, u32[]{:S(2)}, u32[]{:S(2)}) %all-to-all-start.1) | async-done | bytes 2949152 | tf_op jit(solution)/shard_map/all_to_all | solution.py:145
  701.7 6.4 gather_fusion
  708.1 3.9 reshape.116
  712.0 4.0 multiply_reduce_fusion
  (53 shorter events, 7.1 us)
Async XLA Ops:
  6.5 393.6 %copy-start = (bf16[1,384,2880]{1,2,0:T(8,128)(2,1)S(1)}, bf16[1,384,2880]{1,2,0:T(8,128)(2,1)}, u32[]{:S(2)}) copy-start(bf16[1,384,2880]{1,2,0:T(8,128)(2,1)} %param.21) | copy-start | bytes 6635524
  6.5 72.2 %all-gather.2.cloned.1.call-start = ((), (), s32[]{:S(2)}) async-start(), calls=%async_computation.4 | async-start | bytes 7372800 | tf_op jit(solution)/shard_map/all_gather | solution.py:111
  7.3 86.6 %reduce-scatter.3.cloned.1.call-start = ((), (), s32[]{:S(2)}) async-start(), calls=%async_computation.5 | async-start | bytes 2260992 | tf_op jit(solution)/shard_map/reduce_scatter | solution.py:114
  8.8 6.8 collective-permute-start
  78.7 6.1 copy-start.5
  78.7 15.1 %copy-start.3 = (bf16[64,2880]{1,0:T(8,128)(2,1)S(1)}, bf16[64,2880]{1,0:T(8,128)(2,1)}, u32[]{:S(2)}) copy-start(bf16[64,2880]{1,0:T(8,128)(2,1)} %param.14) | copy-start | bytes 1105924
  78.7 16.5 %copy-start.4 = (f32[2880]{0:T(1024)S(1)}, f32[2880]{0:T(1024)}, u32[]{:S(2)}) copy-start(f32[2880]{0:T(1024)} %param.16) | copy-start | bytes 34564
  84.7 538.6 %reduce-scatter.5.cloned.1.call-start = ((), (), s32[]{:S(2)}) async-start(), calls=%async_computation.6 | async-start | bytes 30146560 | tf_op jit(solution)/shard_map/reduce_scatter | solution.py:139
  180.9 69.4 %collective-permute-start.1 = (bf16[8,64,2880]{2,1,0:T(8,128)(2,1)}, bf16[8,64,2880]{2,1,0:T(8,128)(2,1)}, u32[]{:S(2)}, u32[]{:S(2)}) collective-permute-start(bf16[8,64,2880]{2,1,0:T(8,128)(2,1)} %all_to_all.10), channel_id=1, source_target_pairs={{0,2},{2,4},{4,6},{6,0},{1,3},{3,5},{5,7},{7,1},{8,10},{10,12},{12... | collective-permute-start | bytes 8847368 | tf_op jit(solution)/shard_map/ppermute | solution.py:22
  182.4 132.5 %collective-permute-start.2 = (bf16[8,64,2880]{2,1,0:T(8,128)(2,1)}, bf16[8,64,2880]{2,1,0:T(8,128)(2,1)}, u32[]{:S(2)}, u32[]{:S(2)}) collective-permute-start(bf16[8,64,2880]{2,1,0:T(8,128)(2,1)} %all_to_all.10), channel_id=1, source_target_pairs={{0,6},{2,0},{4,2},{6,4},{1,7},{3,1},{5,3},{7,5},{8,14},{10,8},{12,... | collective-permute-start | bytes 8847368 | tf_op jit(solution)/shard_map/ppermute | solution.py:25
  250.3 127.9 %collective-permute-start.3 = (bf16[8,64,2880]{2,1,0:T(8,128)(2,1)}, bf16[8,64,2880]{2,1,0:T(8,128)(2,1)}, u32[]{:S(2)}, u32[]{:S(2)}) collective-permute-start(bf16[8,64,2880]{2,1,0:T(8,128)(2,1)} %collective-permute-done.1), channel_id=1, source_target_pairs={{0,2},{2,4},{4,6},{6,0},{1,3},{3,5},{5,7},{7,1},{8,10},{10,12},{12... | collective-permute-start | bytes 8847368 | tf_op jit(solution)/shard_map/ppermute | solution.py:22
  318.6 63.3 %copy-start.7 = (bf16[1,2880,384]{2,1,0:T(8,128)(2,1)S(1)}, bf16[1,2880,384]{2,1,0:T(8,128)(2,1)}, u32[]{:S(2)}) copy-start(bf16[1,2880,384]{2,1,0:T(8,128)(2,1)} %param.20) | copy-start | bytes 6635524
  381.9 10.8 %copy-start.1 = (bf16[32,64,2880]{2,1,0:T(8,128)(2,1)S(1)}, bf16[32,64,2880]{2,1,0:T(8,128)(2,1)}, u32[]{:S(2)}) copy-start(bf16[32,64,2880]{2,1,0:T(8,128)(2,1)} %constant_dynamic-update-slice_fusion.2) | copy-start | bytes 35389444
  381.9 10.8 %copy-start.8 = (bf16[1,2880,384]{2,1,0:T(8,128)(2,1)S(1)}, bf16[1,2880,384]{2,1,0:T(8,128)(2,1)}, u32[]{:S(2)}) copy-start(bf16[1,2880,384]{2,1,0:T(8,128)(2,1)} %param.19) | copy-start | bytes 6635524
  628.1 4.8 copy-start.6
  628.1 73.5 %all-to-all-start.1 = ((bf16[8,64,2880]{2,1,0:T(8,128)(2,1)}), bf16[8,64,2880]{2,1,0:T(8,128)(2,1)}, u32[]{:S(2)}, u32[]{:S(2)}) async-start(bf16[8,64,2880]{2,1,0:T(8,128)(2,1)} %convert_element_type.48), calls=%async_computation.3 | async-start | bytes 6029312 | tf_op jit(solution)/shard_map/all_to_all | solution.py:145
  712.0 4.0 copy-start.2
Sparse Core Ops, SparseCore 0:
  9.2 69.4 all-gather.1
  84.8 8.9 reduce-scatter.2
  411.7 211.5 reduce-scatter.4
